TPU v7x, 128 devices: a whole 4x4x4 slice. The times are simulated.
128 devices in a mesh: slab: 16 (over z, y_hi, core), deal: 8 (over x, y_lo).
Axes of the slice: x: 4, y: 4 (y_hi: 2, y_lo: 2; y = y_hi * 2 + y_lo), z: 4, core: 2. Of those that a mesh axis runs over, the one named last changes fastest.
Arguments:
- offsets: float32 [131072, 3, 128], P(('slab', 'deal')), may hold values from -0.5 to 0.5
- velocity: float32 [131072, 3, 128], P(('slab', 'deal')), may hold values from -6 to 6
- affine: float32 [131072, 9, 128], P(('slab', 'deal')), may hold values from -6 to 6
- particle_mass: float32 [131072, 128], P(('slab', 'deal')), may hold values from 0.5 to 2
- cell_in_tile: int32 [131072, 128], P(('slab', 'deal')), may hold values from 0 to 255
- block_tile: int32 [131072], P(('slab', 'deal')), may hold values from 0 to 2047, as said below
- live_blocks: int32 [16, 8], P('slab', 'deal'), may hold values from 512 to 1024, as said below
- send_lists: int32 [16, 8, 2, 16], P('slab', 'deal'), may hold values from 0 to 1023, as said below
- send_counts: int32 [16, 8, 2], P('slab', 'deal'), may hold values from 0 to 16, as said below
Outputs:
- updated_particles: float32 [131072, 15, 128], P(('slab', 'deal'))
- arrivals: float32 [16, 8, 2, 16, 16, 128], P('slab', 'deal')
- grid_velocity: float32 [3, 1024, 8192], P(None, 'slab', 'deal')
Inputs may be any that keep to these rules, and one draw needn't show every extreme that they name: `block_tile`: blocks are sorted by cell: on device (s, d) the tiles never fall along its blocks and lie in [max(d * R - M, 0), min((d + 1) * R + M, 2048)) with R = 256 and M = max(R // 16, 1); some device with d > 0 reaches d * R - M. `live_blocks`: some device has all 1024 blocks live. `send_lists`: the 32 entries of one device's two lists are distinct blocks of that device. `send_counts`: counts toward a slab beyond the ends are zero; some device sends 16 blocks downslope.
All inputs are finite; a program needn't handle non-finite values.
Results may differ from a plain program's by a relative error of at most 0.000073.
Values sent between devices are 32-bit elements; how exact they have to be, the bound alone decides.
No kernel may reach another device: no remote copies, remote signals or barrier semaphores. Data moves between devices by JAX's collectives and lax.ppermute only.
A program may use at most 128 MiB of HBM per device.

v0:
```python
import math
import jax
import jax.numpy as jnp
from jax import lax
from jax.sharding import PartitionSpec as P

PX = 64
PLANE = 8192
TILE = 256
time_step = 0.1
viscosity = 0.2
gravity_pull = (3.0, 0.0, -5.0)


def extended(x, sides, width):
    for axis, dim in sides:
        count, length = (lax.axis_size(axis), x.shape[dim])
        up = [(i, (i + 1) % count) for i in range(count - 1)]
        down = [(j, i) for i, j in up]
        last = lax.slice_in_dim(x, length - width, length, axis=dim)
        initial = lax.slice_in_dim(x, 0, width, axis=dim)
        before = lax.ppermute(last, axis, up)
        after = lax.ppermute(initial, axis, down)
        x = jnp.concatenate([before, x, after], axis=dim)
    return x


def from_behind(x, axis, by):
    count = lax.axis_size(axis)
    pairs = [(i, i + by) for i in range(count) if 0 <= i + by < count]
    return lax.ppermute(x, axis, pairs)


def momentum(offsets, velocity, affine):
    columns = []
    for column in range(3):
        total = velocity[:, column]
        for inner in range(3):
            total = total - affine[:, 3 * column + inner] * offsets[:, inner]
        columns.append(total)
    return jnp.stack(columns, axis=1)


def grid_update(summed):
    floor_mass = jnp.maximum(summed[0], 1.0)
    speeds = []
    for column in range(3):
        speeds.append(summed[1 + column] / floor_mass + time_step * gravity_pull[column])
    return jnp.stack(speeds, axis=0)


def smooth_planes(speed):
    padded = extended(speed, (("slab", 1),), 1)
    return speed + viscosity * (padded[:, 2:] + padded[:, :-2] - 2.0 * speed)


def new_state(offsets, moved):
    shifted = offsets + time_step * moved
    affine_rows = []
    for column in range(3):
        for inner in range(3):
            affine_rows.append(-4.0 * moved[:, column] * offsets[:, inner])
    return jnp.concatenate([shifted, moved, jnp.stack(affine_rows, axis=1)], axis=1)


def body(
    offsets,
    velocity,
    affine,
    particle_mass,
    cell_in_tile,
    block_tile,
    live_blocks,
    send_lists,
    send_counts,
):
    highest = lax.Precision.HIGHEST
    blocks_here = offsets.shape[0]
    deal_count = lax.axis_size("deal")
    deal_index = lax.axis_index("deal")
    tile_count = PX * PLANE // TILE
    active = (jnp.arange(blocks_here, dtype=jnp.int32) < live_blocks[0, 0]).astype(jnp.float32)
    weight = particle_mass * active[:, None]
    moment = momentum(offsets, velocity, affine)
    deposit = jnp.concatenate([weight[:, None, :], weight[:, None, :] * moment], axis=1)
    group_size = math.gcd(blocks_here, 128)
    group_count = blocks_here // group_size
    grouped_deposit = deposit.reshape(group_count, group_size, 4, 128)
    grouped_cells = cell_in_tile.reshape(group_count, group_size, 128)
    grouped_tiles = block_tile.reshape(group_count, group_size)
    tile_slots = jnp.arange(TILE, dtype=jnp.int32)
    tile_labels = jnp.arange(tile_count, dtype=jnp.int32)

    def scatter_group(accumulated, pieces):
        part_deposit, part_cells, part_tiles = pieces
        selector = (part_cells[:, :, None] == tile_slots).astype(jnp.float32)
        per_block = jnp.einsum("bcp,bpk->bck", part_deposit, selector, precision=highest)
        placing = (part_tiles[:, None] == tile_labels).astype(jnp.float32)
        return (
            accumulated + jnp.einsum("bt,bck->ctk", placing, per_block, precision=highest),
            None,
        )

    start_grid = jnp.zeros((4, tile_count, TILE), jnp.float32)
    accumulated, unused = lax.scan(
        scatter_group, start_grid, (grouped_deposit, grouped_cells, grouped_tiles)
    )
    partial_grid = accumulated.reshape(4, PX, PLANE)
    share_width = PLANE // deal_count
    summed = lax.psum(partial_grid, "deal")
    settled = smooth_planes(grid_update(summed))
    own_share = lax.dynamic_slice_in_dim(settled, deal_index * share_width, share_width, 2)
    tiles_view = settled.reshape(3, tile_count, TILE)

    def gather_group(pieces):
        part_cells, part_tiles = pieces
        selector = (part_cells[:, :, None] == tile_slots).astype(jnp.float32)
        chosen = jnp.take(tiles_view, part_tiles, axis=1)
        return jnp.einsum("cbk,bpk->bcp", chosen, selector, precision=highest)

    moved = lax.map(gather_group, (grouped_cells, grouped_tiles)).reshape(blocks_here, 3, 128)
    state = new_state(offsets, moved)
    records = jnp.concatenate([state, particle_mass[:, None, :]], axis=1)
    lists_here = send_lists[0, 0]
    counts_here = send_counts[0, 0]
    mig_slots = lists_here.shape[1]
    leaving = records[lists_here]
    keeping = (jnp.arange(mig_slots, dtype=jnp.int32)[None, :] < counts_here[:, None]).astype(
        jnp.float32
    )
    leaving = leaving * keeping[:, :, None, None]
    from_left = from_behind(leaving[0], "slab", 1)
    from_right = from_behind(leaving[1], "slab", -1)
    arrivals = jnp.stack([from_left, from_right], axis=0)[None, None]
    return (state, arrivals, own_share)


def solution(mesh):
    placed = (
        P(("slab", "deal"), None, None),
        P(("slab", "deal"), None, None),
        P(("slab", "deal"), None, None),
        P(("slab", "deal"), None),
        P(("slab", "deal"), None),
        P(("slab", "deal")),
        P("slab", "deal"),
        P("slab", "deal", None, None),
        P("slab", "deal", None),
    )
    return jax.shard_map(
        body,
        mesh=mesh,
        in_specs=placed,
        out_specs=(
            P(("slab", "deal"), None, None),
            P("slab", "deal", None, None, None, None),
            P(None, "slab", "deal"),
        ),
        check_vma=False,
    )
```

profile of v0, /device:TPU:36, one launch (start us, length us, event | category | flops | bytes accessed | tf_op | source)
XLA Modules:
  0.0 715.3 jit_solution(17750326959352518418)
XLA Ops:
  17.1 127.7 %while.23 = (s32[]{:T(128)}, f32[4,2048,256]{1,2,0:T(8,128)}, f32[8,128,4,128]{3,2,1,0:T(4,128)}, s32[8,128,128]{2,1,0:T(8,128)}, s32[8,128]{1,0:T(8,128)}, /*index=5*/s32[]{:T(128)}, s32[]{:T(128)}) while((s32[]{:T(128)}, f32[4,2048,256]{1,2,0:T(8,128)}, f32[8,128,4,128]{3,2,1,0:T(4,128)}, s32[8,128,128]{2,1,0:T(8,128)}, ...), condition=%wide.region_1.2_spmd.clone, body=%wide.region_0.1_spmd.clone.sunk | while | flops 3431202816 | bytes 18286184 | solution.py:105
  18.7 6.5 fusion.76
  32.7 6.5 fusion.76
  39.2 8.2 %bitcast_add_fusion.2 = f32[4,2048,256]{1,2,0:T(8,128)} fusion(f32[4,2048,256]{1,2,0:T(8,128)} %get-tuple-element.245, pred[]{:T(512)S(6)} %compare.3, f32[128,4,256]{2,1,0:T(4,128)S(1)} %fusion.76, s32[128]{0:T(128)S(1)} %fusion.77), kind=kOutput, calls=%fused_computation.24.clone.1 | convolution fusion | flops 3225681920 | bytes 17302016 | tf_op jit(solution)/shard_map/while/body/eval_jaxpr/bt,bck->ctk/dot_general | solution.py:100
  49.0 6.5 fusion.76
  55.5 8.2 %bitcast_add_fusion.2 = f32[4,2048,256]{1,2,0:T(8,128)} fusion(f32[4,2048,256]{1,2,0:T(8,128)} %get-tuple-element.245, pred[]{:T(512)S(6)} %compare.3, f32[128,4,256]{2,1,0:T(4,128)S(1)} %fusion.76, s32[128]{0:T(128)S(1)} %fusion.77), kind=kOutput, calls=%fused_computation.24.clone.1 | convolution fusion | flops 3225681920 | bytes 17302016 | tf_op jit(solution)/shard_map/while/body/eval_jaxpr/bt,bck->ctk/dot_general | solution.py:100
  65.2 6.5 fusion.76
  71.7 8.2 %bitcast_add_fusion.2 = f32[4,2048,256]{1,2,0:T(8,128)} fusion(f32[4,2048,256]{1,2,0:T(8,128)} %get-tuple-element.245, pred[]{:T(512)S(6)} %compare.3, f32[128,4,256]{2,1,0:T(4,128)S(1)} %fusion.76, s32[128]{0:T(128)S(1)} %fusion.77), kind=kOutput, calls=%fused_computation.24.clone.1 | convolution fusion | flops 3225681920 | bytes 17302016 | tf_op jit(solution)/shard_map/while/body/eval_jaxpr/bt,bck->ctk/dot_general | solution.py:100
  81.5 6.5 fusion.76
  87.9 8.2 %bitcast_add_fusion.2 = f32[4,2048,256]{1,2,0:T(8,128)} fusion(f32[4,2048,256]{1,2,0:T(8,128)} %get-tuple-element.245, pred[]{:T(512)S(6)} %compare.3, f32[128,4,256]{2,1,0:T(4,128)S(1)} %fusion.76, s32[128]{0:T(128)S(1)} %fusion.77), kind=kOutput, calls=%fused_computation.24.clone.1 | convolution fusion | flops 3225681920 | bytes 17302016 | tf_op jit(solution)/shard_map/while/body/eval_jaxpr/bt,bck->ctk/dot_general | solution.py:100
  97.7 6.5 fusion.76
  104.2 8.2 %bitcast_add_fusion.2 = f32[4,2048,256]{1,2,0:T(8,128)} fusion(f32[4,2048,256]{1,2,0:T(8,128)} %get-tuple-element.245, pred[]{:T(512)S(6)} %compare.3, f32[128,4,256]{2,1,0:T(4,128)S(1)} %fusion.76, s32[128]{0:T(128)S(1)} %fusion.77), kind=kOutput, calls=%fused_computation.24.clone.1 | convolution fusion | flops 3225681920 | bytes 17302016 | tf_op jit(solution)/shard_map/while/body/eval_jaxpr/bt,bck->ctk/dot_general | solution.py:100
  113.9 6.5 fusion.76
  120.4 8.2 %bitcast_add_fusion.2 = f32[4,2048,256]{1,2,0:T(8,128)} fusion(f32[4,2048,256]{1,2,0:T(8,128)} %get-tuple-element.245, pred[]{:T(512)S(6)} %compare.3, f32[128,4,256]{2,1,0:T(4,128)S(1)} %fusion.76, s32[128]{0:T(128)S(1)} %fusion.77), kind=kOutput, calls=%fused_computation.24.clone.1 | convolution fusion | flops 3225681920 | bytes 17302016 | tf_op jit(solution)/shard_map/while/body/eval_jaxpr/bt,bck->ctk/dot_general | solution.py:100
  130.2 6.5 fusion.76
  136.7 8.2 %bitcast_add_fusion.2 = f32[4,2048,256]{1,2,0:T(8,128)} fusion(f32[4,2048,256]{1,2,0:T(8,128)} %get-tuple-element.245, pred[]{:T(512)S(6)} %compare.3, f32[128,4,256]{2,1,0:T(4,128)S(1)} %fusion.76, s32[128]{0:T(128)S(1)} %fusion.77), kind=kOutput, calls=%fused_computation.24.clone.1 | convolution fusion | flops 3225681920 | bytes 17302016 | tf_op jit(solution)/shard_map/while/body/eval_jaxpr/bt,bck->ctk/dot_general | solution.py:100
  144.9 8.7 %copy.94 = f32[4,2048,256]{2,1,0:T(8,128)} copy(f32[4,2048,256]{1,2,0:T(8,128)} %get-tuple-element.72) | data formatting | bytes 16777216 | tf_op jit(solution)/shard_map/while | solution.py:105
  153.6 9.4 %reshape.134 = f32[4,64,8192]{2,1,0:T(8,128)} reshape(f32[4,2048,256]{2,1,0:T(8,128)} %copy.94) | data formatting | bytes 16777216 | tf_op jit(solution)/shard_map/reshape | solution.py:108
  163.8 344.7 %all-reduce.2.cloned.1.call-done = f32[4,64,8192]{2,1,0:T(8,128)} async-done(((f32[4,64,8192]{2,1,0:T(8,128)}), f32[4,64,8192]{2,1,0:T(8,128)}) %all-reduce.2.cloned.1.call-update) | async-done | bytes 8388624 | tf_op jit(solution)/shard_map/psum | solution.py:110
  515.7 6.2 collective-permute-start
  528.8 7.1 reshape.135
  535.8 10.7 %copy.99 = f32[3,2048,256]{2,0,1:T(4,128)} copy(f32[3,2048,256]{2,1,0:T(8,128)} %reshape.135) | data formatting | bytes 12582912
  546.5 130.2 %while.22 = (s32[]{:T(128)}, f32[8,128,3,128]{3,1,0,2:T(8,128)S(1)}, s32[8,128]{1,0:T(8,128)}, f32[3,2048,256]{2,0,1:T(4,128)}, s32[8,128,128]{2,1,0:T(8,128)}, /*index=5*/s32[]{:T(128)}) while((s32[]{:T(128)}, f32[8,128,3,128]{3,1,0,2:T(8,128)S(1)}, s32[8,128]{1,0:T(8,128)}, f32[3,2048,256]{2,0,1:T(4,128)}, ...), condition=%wide.region_4.5_spmd.clone, body=%wide.region_3.4_spmd.clone.sunk | while | flops 155289728 | bytes 2038621 | solution.py:121
  553.9 8.9 %fusion.72 = f32[1,128,3,128]{3,2,1,0:T(4,128)S(1)} fusion(s32[128,128]{1,0:T(8,128)S(1)} %dynamic-slice_bitcast_fusion.4, f32[128,3,256]{2,1,0:T(4,128)} %gather_fusion, pred[128]{0:T(512)(128)(4,1)S(1)} %compare_and_fusion.2), kind=kOutput, calls=%fused_computation.8.clone.1 | convolution fusion | flops 155287552 | bytes 655488 | tf_op jit(solution)/shard_map/while/body/eval_jaxpr/cbk,bpk->bcp/dot_general | solution.py:119
  570.2 8.9 %fusion.72 = f32[1,128,3,128]{3,2,1,0:T(4,128)S(1)} fusion(s32[128,128]{1,0:T(8,128)S(1)} %dynamic-slice_bitcast_fusion.4, f32[128,3,256]{2,1,0:T(4,128)} %gather_fusion, pred[128]{0:T(512)(128)(4,1)S(1)} %compare_and_fusion.2), kind=kOutput, calls=%fused_computation.8.clone.1 | convolution fusion | flops 155287552 | bytes 655488 | tf_op jit(solution)/shard_map/while/body/eval_jaxpr/cbk,bpk->bcp/dot_general | solution.py:119
  586.5 8.9 %fusion.72 = f32[1,128,3,128]{3,2,1,0:T(4,128)S(1)} fusion(s32[128,128]{1,0:T(8,128)S(1)} %dynamic-slice_bitcast_fusion.4, f32[128,3,256]{2,1,0:T(4,128)} %gather_fusion, pred[128]{0:T(512)(128)(4,1)S(1)} %compare_and_fusion.2), kind=kOutput, calls=%fused_computation.8.clone.1 | convolution fusion | flops 155287552 | bytes 655488 | tf_op jit(solution)/shard_map/while/body/eval_jaxpr/cbk,bpk->bcp/dot_general | solution.py:119
  602.7 8.9 %fusion.72 = f32[1,128,3,128]{3,2,1,0:T(4,128)S(1)} fusion(s32[128,128]{1,0:T(8,128)S(1)} %dynamic-slice_bitcast_fusion.4, f32[128,3,256]{2,1,0:T(4,128)} %gather_fusion, pred[128]{0:T(512)(128)(4,1)S(1)} %compare_and_fusion.2), kind=kOutput, calls=%fused_computation.8.clone.1 | convolution fusion | flops 155287552 | bytes 655488 | tf_op jit(solution)/shard_map/while/body/eval_jaxpr/cbk,bpk->bcp/dot_general | solution.py:119
  619.0 8.9 %fusion.72 = f32[1,128,3,128]{3,2,1,0:T(4,128)S(1)} fusion(s32[128,128]{1,0:T(8,128)S(1)} %dynamic-slice_bitcast_fusion.4, f32[128,3,256]{2,1,0:T(4,128)} %gather_fusion, pred[128]{0:T(512)(128)(4,1)S(1)} %compare_and_fusion.2), kind=kOutput, calls=%fused_computation.8.clone.1 | convolution fusion | flops 155287552 | bytes 655488 | tf_op jit(solution)/shard_map/while/body/eval_jaxpr/cbk,bpk->bcp/dot_general | solution.py:119
  635.2 8.9 %fusion.72 = f32[1,128,3,128]{3,2,1,0:T(4,128)S(1)} fusion(s32[128,128]{1,0:T(8,128)S(1)} %dynamic-slice_bitcast_fusion.4, f32[128,3,256]{2,1,0:T(4,128)} %gather_fusion, pred[128]{0:T(512)(128)(4,1)S(1)} %compare_and_fusion.2), kind=kOutput, calls=%fused_computation.8.clone.1 | convolution fusion | flops 155287552 | bytes 655488 | tf_op jit(solution)/shard_map/while/body/eval_jaxpr/cbk,bpk->bcp/dot_general | solution.py:119
  651.5 8.9 %fusion.72 = f32[1,128,3,128]{3,2,1,0:T(4,128)S(1)} fusion(s32[128,128]{1,0:T(8,128)S(1)} %dynamic-slice_bitcast_fusion.4, f32[128,3,256]{2,1,0:T(4,128)} %gather_fusion, pred[128]{0:T(512)(128)(4,1)S(1)} %compare_and_fusion.2), kind=kOutput, calls=%fused_computation.8.clone.1 | convolution fusion | flops 155287552 | bytes 655488 | tf_op jit(solution)/shard_map/while/body/eval_jaxpr/cbk,bpk->bcp/dot_general | solution.py:119
  667.8 8.9 %fusion.72 = f32[1,128,3,128]{3,2,1,0:T(4,128)S(1)} fusion(s32[128,128]{1,0:T(8,128)S(1)} %dynamic-slice_bitcast_fusion.4, f32[128,3,256]{2,1,0:T(4,128)} %gather_fusion, pred[128]{0:T(512)(128)(4,1)S(1)} %compare_and_fusion.2), kind=kOutput, calls=%fused_computation.8.clone.1 | convolution fusion | flops 155287552 | bytes 655488 | tf_op jit(solution)/shard_map/while/body/eval_jaxpr/cbk,bpk->bcp/dot_general | solution.py:119
  681.9 8.1 %copy.101 = f32[1024,16,128]{2,1,0:T(8,128)} copy(f32[1024,16,128]{2,0,1:T(8,128)S(1)} %get-tuple-element.173) | data formatting | bytes 16777216 | tf_op jit(solution)/shard_map/concatenate | solution.py:123
  (127 shorter events, 124.4 us)
Async XLA Ops:
  7.2 5.8 copy-start.1
  7.2 501.4 %all-reduce.2.cloned.1.call-start = ((), (), s32[]{:S(2)}) async-start(), calls=%async_computation | async-start | bytes 16777216 | tf_op jit(solution)/shard_map/psum | solution.py:110
  163.0 0.7 copy-start.4
  163.0 0.8 copy-start.5
  513.8 9.2 %collective-permute-start.1 = (f32[3,1,8192]{2,0,1:T(4,128)S(1)}, f32[3,1,8192]{2,0,1:T(4,128)S(1)}, u32[]{:S(2)}, u32[]{:S(2)}) collective-permute-start(f32[3,1,8192]{2,0,1:T(4,128)S(1)} %copy.97), channel_id=1, source_target_pairs={{0,8},{8,16},{16,24},{24,32},{32,40},{40,48},{48,56},{56,64},{64,7... | collective-permute-start | bytes 294920 | tf_op jit(solution)/shard_map/ppermute | solution.py:22
  515.7 8.6 %collective-permute-start = (f32[3,1,8192]{2,0,1:T(4,128)S(1)}, f32[3,1,8192]{2,0,1:T(4,128)S(1)}, u32[]{:S(2)}, u32[]{:S(2)}) collective-permute-start(f32[3,1,8192]{2,0,1:T(4,128)S(1)} %copy.95), channel_id=1, source_target_pairs={{8,0},{16,8},{24,16},{32,24},{40,32},{48,40},{56,48},{64,56},{72,6... | collective-permute-start | bytes 294920 | tf_op jit(solution)/shard_map/ppermute | solution.py:23
  546.5 130.2 %copy-start = (f32[1024,3,128]{2,0,1:T(8,128)S(1)}, f32[1024,3,128]{2,0,1:T(8,128)}, u32[]{:S(2)}) copy-start(f32[1024,3,128]{2,0,1:T(8,128)} %param.13) | copy-start | bytes 4718596
  677.5 1.0 copy-start.2
  678.7 3.2 copy-start.3
  694.1 13.6 %collective-permute-start.2 = (f32[16,16,128]{2,1,0:T(8,128)S(1)}, f32[16,16,128]{2,1,0:T(8,128)S(1)}, u32[]{:S(2)}, u32[]{:S(2)}) collective-permute-start(f32[16,16,128]{2,1,0:T(8,128)S(1)} %get-tuple-element.171), channel_id=1, source_target_pairs={{0,8},{8,16},{16,24},{24,32},{32,40},{40,48},{48,56},{56,64},{64,7... | collective-permute-start | bytes 393224 | tf_op jit(solution)/shard_map/ppermute | solution.py:31
  696.0 11.7 %collective-permute-start.3 = (f32[16,16,128]{2,1,0:T(8,128)S(1)}, f32[16,16,128]{2,1,0:T(8,128)S(1)}, u32[]{:S(2)}, u32[]{:S(2)}) collective-permute-start(f32[16,16,128]{2,1,0:T(8,128)S(1)} %get-tuple-element.172), channel_id=1, source_target_pairs={{8,0},{16,8},{24,16},{32,24},{40,32},{48,40},{56,48},{64,56},{72,6... | collective-permute-start | bytes 393224 | tf_op jit(solution)/shard_map/ppermute | solution.py:31
Sparse Core Ops, SparseCore 0:
  163.1 345.3 all-reduce.1
where the time goes:
time: 718 us; the launch traced here: 715 us
  waiting for transfers between devices  347 us (48%)
  matrix products  187 us (26%)
  local copies, waits for them, and re-layouts  115 us (16%)
  other arithmetic  35.2 us (5%)
  starting transfers between devices  16.3 us (2%)
  between operations  15 us (2%)
    psum x1, waiting for transfers between devices, body(): summed = lax.psum(partial_grid, 'deal')  345 us
    dot_general x8, matrix products, gather_group(): return jnp.einsum('cbk,bpk->bcp', chosen, selector, precision=highest)  71.3 us
    dot_general x8, matrix products, scatter_group(): jnp.einsum('bt,bck->ctk', placing, per_block, precision=highest)  63.6 us
    dot_general x8, matrix products, scatter_group(): jnp.einsum('bcp,bpk->bck', part_deposit, selector, precision=highest)  51.9 us
    gather x8, local copies, waits for them, and re-layouts, gather_group(): chosen = jnp.take(tiles_view, part_tiles, axis=1)  40.3 us
    unnamed x14, local copies, waits for them, and re-layouts  15.4 us
  transfers between devices with their start and end apart: 5, of which 3 were waited for; matrix products, arithmetic and copies ran while one was open for 1% of the time, Pallas kernels for 0%

commit v1 on v0

--- a/solution.py
+++ b/solution.py
@@ -74,6 +74,10 @@
     send_lists,
     send_counts,
 ):
+
+    def press_array_for(block_here):
+        return jnp.sum(lax.all_gather(block_here, axis_name="deal"), 0)
+
     highest = lax.Precision.HIGHEST
     blocks_here = offsets.shape[0]
     deal_count = lax.axis_size("deal")
@@ -107,7 +111,7 @@
     )
     partial_grid = accumulated.reshape(4, PX, PLANE)
     share_width = PLANE // deal_count
-    summed = lax.psum(partial_grid, "deal")
+    summed = press_array_for(partial_grid)
     settled = smooth_planes(grid_update(summed))
     own_share = lax.dynamic_slice_in_dim(settled, deal_index * share_width, share_width, 2)
     tiles_view = settled.reshape(3, tile_count, TILE)

time: 718 us -> 1670 us (2.33)
  waiting for transfers between devices: 347 us -> 1280 us
  other arithmetic: 35.2 us -> 60.9 us
    all_gather x0 -> x1, waiting for transfers between devices: none -> 1270 us  [press_array_for(): return jnp.sum(lax.all_gather(block_here, axis_name='deal'), 0)]
    psum x1 -> x0, waiting for transfers between devices: 345 us -> none  [body(): summed = lax.psum(partial_grid, 'deal')]
    reduce_sum x0 -> x1, other arithmetic: none -> 24.4 us  [press_array_for(): return jnp.sum(lax.all_gather(block_here, axis_name='deal'), 0)]
  transfers between devices with their start and end apart: 5 -> 5, of which waited for: 3 -> 3; matrix products, arithmetic and copies ran while one was open for 1% -> 0% of each run, Pallas kernels for 0% -> 0%
where the time goes in v1:
time: 1670 us
  waiting for transfers between devices  1280 us (77%)
  matrix products  187 us (11%)
  local copies, waits for them, and re-layouts  115 us (7%)
  other arithmetic  60.9 us (4%)
    all_gather x1, waiting for transfers between devices, press_array_for(): return jnp.sum(lax.all_gather(block_here, axis_name='deal'), 0)  1270 us
    dot_general x8, matrix products, gather_group(): return jnp.einsum('cbk,bpk->bcp', chosen, selector, precision=highest)  71.3 us
    dot_general x8, matrix products, scatter_group(): jnp.einsum('bt,bck->ctk', placing, per_block, precision=highest)  63.8 us
    dot_general x8, matrix products, scatter_group(): jnp.einsum('bcp,bpk->bck', part_deposit, selector, precision=highest)  51.9 us
    gather x8, local copies, waits for them, and re-layouts, gather_group(): chosen = jnp.take(tiles_view, part_tiles, axis=1)  40.3 us
  transfers between devices with their start and end apart: 5, of which 3 were waited for; matrix products, arithmetic and copies ran while one was open for 0% of the time, Pallas kernels for 0%

profile of v1, /device:TPU:36, one launch (start us, length us, event | category | flops | bytes accessed | tf_op | source)
XLA Modules:
  0.0 1669.5 jit_solution(1526120779859189258)
XLA Ops:
  18.6 128.0 %while.23 = (s32[]{:T(128)}, f32[4,2048,256]{1,2,0:T(8,128)}, f32[8,128,4,128]{3,2,1,0:T(4,128)}, s32[8,128,128]{2,1,0:T(8,128)}, s32[8,128]{1,0:T(8,128)}, /*index=5*/s32[]{:T(128)}, s32[]{:T(128)}) while((s32[]{:T(128)}, f32[4,2048,256]{1,2,0:T(8,128)}, f32[8,128,4,128]{3,2,1,0:T(4,128)}, s32[8,128,128]{2,1,0:T(8,128)}, ...), condition=%wide.region_1.2_spmd.clone, body=%wide.region_0.1_spmd.clone.sunk | while | flops 3431202816 | bytes 18286684 | solution.py:109
  19.5 6.5 fusion.76
  33.6 6.5 fusion.76
  40.7 8.2 bitcast_add_fusion.2
  49.8 6.5 fusion.76
  57.0 8.2 bitcast_add_fusion.2
  66.1 6.5 fusion.76
  73.3 8.3 bitcast_add_fusion.2
  82.4 6.5 fusion.76
  89.6 8.2 bitcast_add_fusion.2
  98.7 6.5 fusion.76
  105.9 8.2 bitcast_add_fusion.2
  114.9 6.5 fusion.76
  122.1 8.2 bitcast_add_fusion.2
  131.2 6.5 fusion.76
  138.4 8.2 bitcast_add_fusion.2
  146.7 8.7 copy.94
  155.4 9.4 all_gather_reshape.3
  165.6 1270.7 %all-gather.2.cloned.1.call-done = f32[8,4,64,8192]{3,2,1,0:T(8,128)} async-done(((f32[1,4,64,8192]{3,2,1,0:T(8,128)}), f32[8,4,64,8192]{3,2,1,0:T(8,128)}) %all-gather.2.cloned.1.call-update) | async-done | bytes 67108880 | tf_op jit(solution)/shard_map/all_gather | solution.py:79
  1436.3 24.4 %reduce_sum.9 = f32[4,64,8192]{2,1,0:T(8,128)} reduce(f32[8,4,64,8192]{3,2,1,0:T(8,128)} %all-gather.2.cloned.1.call-done, f32[]{:T(128)} %constant.31.clone.1), dimensions={0}, to_apply=%region_2.3 | reduce | flops 14680064 | bytes 75497472 | tf_op jit(solution)/shard_map/reduce_sum | solution.py:79
  1483.3 7.1 reshape.131
  1490.4 10.7 copy.99
  1501.1 130.0 %while.22 = (s32[]{:T(128)}, f32[8,128,3,128]{3,1,0,2:T(8,128)S(1)}, s32[8,128]{1,0:T(8,128)}, f32[3,2048,256]{2,0,1:T(4,128)}, s32[8,128,128]{2,1,0:T(8,128)}, /*index=5*/s32[]{:T(128)}) while((s32[]{:T(128)}, f32[8,128,3,128]{3,1,0,2:T(8,128)S(1)}, s32[8,128]{1,0:T(8,128)}, f32[3,2048,256]{2,0,1:T(4,128)}, ...), condition=%wide.region_4.5_spmd.clone, body=%wide.region_3.4_spmd.clone.sunk | while | flops 155289728 | bytes 2038613 | solution.py:125
  1508.3 8.9 fusion.72
  1524.6 8.9 fusion.72
  1540.9 8.9 fusion.72
  1557.1 8.9 fusion.72
  1573.4 8.9 fusion.72
  1589.6 8.9 fusion.72
  1605.9 8.9 fusion.72
  1622.1 8.9 fusion.72
  1636.3 8.1 copy.101
  (128 shorter events, 134.3 us)
Async XLA Ops:
  7.2 3.1 copy-start
  7.2 6.3 copy-start.1
  7.2 1429.1 %all-gather.2.cloned.1.call-start = ((), (), s32[]{:S(2)}) async-start(), calls=%async_computation | async-start | bytes 75497472 | tf_op jit(solution)/shard_map/all_gather | solution.py:79
  164.8 0.7 copy-start.4
  164.8 0.8 copy-start.5
  1465.9 6.7 collective-permute-start
  1470.1 8.7 collective-permute-start.1
  1631.8 1.0 copy-start.2
  1633.0 3.2 copy-start.3
  1648.4 13.5 collective-permute-start.2
  1650.4 11.5 collective-permute-start.3
Sparse Core Ops, SparseCore 0:
  164.9 1271.3 all-gather.1
